TPU v7x, 32 devices: a whole 2x2x4 slice. The times are simulated.
32 devices in a mesh: sky: 8 (over z, y), band: 4 (over x, core).
Axes of the slice: x: 2, y: 2, z: 4, core: 2. Of those that a mesh axis runs over, the one named last changes fastest.
Arguments:
- exposures: bfloat16 [8, 4, 1024, 1024], P('sky', 'band'), may hold values from -6 to 6
- inv_variance: bfloat16 [8, 4, 1024, 1024], P('sky', 'band'), may hold values from 0.25 to 4
- mask_planes: int32 [8, 4, 2, 35], P('sky', 'band'), may hold values from 0 to 1073741823, as said below
- sky_columns: int32 [8, 4, 8], replicated, may hold values from 0 to 7, as said below
- basis_rows: float32 [9, 25], replicated, may hold values from -1 to 1
- basis_cols: float32 [9, 25], replicated, may hold values from -1 to 1
- match_coeffs: float32 [8, 4, 9], P('sky', 'band'), may hold values from -2 to 2
- detect_taps: float32 [4, 31], P('band'), may hold values from 0.05 to 0.3
Outputs:
- difference: bfloat16 [8, 4, 1024, 1024], P('sky', 'band')
- detection: float32 [1024, 1024], P('band', 'sky')
Inputs may be any that keep to these rules, and one draw needn't show every extreme that they name: Each row sky_columns[e, b] holds 8 consecutive sky tile columns in order, counted modulo 8; every sky tile column is covered by some exposure of every band. Bit j of mask_planes[e, b, 0, w] marks pixel column 30 w + j of that exposure as bad and bit j of mask_planes[e, b, 1, w] pixel row 30 w + j; bits past 1024 are ignored. In every draw some word has all 30 bits set.
All inputs are finite; a program needn't handle non-finite values.
Results may differ from a plain program's by a relative error of at most 0.0095.
Values may be sent and summed in bfloat16 or wider, within the bound.
No kernel may reach another device: no remote copies, remote signals or barrier semaphores. Data moves between devices by JAX's collectives and lax.ppermute only.
A program may use at most 128 MiB of HBM per device.

v0:
```python
import jax
import jax.numpy as jnp
from jax import lax
from jax.sharding import PartitionSpec as P

TILE = 128
NB = 9
TAPS = 25
DTAPS = 31


def with_halo(block, sides, width):
    for axis, dim in sides:
        count = lax.axis_size(axis)
        forward = [(i, i + 1) for i in range(count - 1)]
        forward.append((count - 1, 0))
        backward = [(target, source) for source, target in forward]
        low = lax.ppermute(
            lax.slice_in_dim(block, block.shape[dim] - width, None, axis=dim), axis, forward
        )
        high = lax.ppermute(lax.slice_in_dim(block, 0, width, axis=dim), axis, backward)
        block = jnp.concatenate([low, block, high], axis=dim)
    return block


def band_matrix(tap_rows, window_width):
    offsets = (
        jnp.arange(window_width, dtype=jnp.int32)[:, None]
        - jnp.arange(TILE, dtype=jnp.int32)[None, :]
    )
    selector = (
        offsets[:, :, None] == jnp.arange(tap_rows.shape[1], dtype=jnp.int32)[None, None, :]
    ).astype(jnp.float32)
    return jnp.einsum(
        "wtl,kl->kwt", selector, tap_rows.astype(jnp.float32), precision=lax.Precision.HIGHEST
    ).astype(jnp.bfloat16)


def keep_pixels(planes, side_length):
    places = jnp.arange(side_length, dtype=jnp.int32)
    column_bits = jnp.bitwise_and(jnp.right_shift(planes[0][places // 30], places % 30), 1)
    row_bits = jnp.bitwise_and(jnp.right_shift(planes[1][places // 30], places % 30), 1)
    return jnp.logical_and(row_bits[:, None] == 0, column_bits[None, :] == 0)


def psf_match(picture, column_taps, row_taps):
    side_length = picture.shape[1]
    block_count = side_length // TILE
    margin = TAPS // 2
    width_full = TILE + 2 * margin
    padded = jnp.pad(picture, ((0, 0), (margin, margin)))
    blocks = jnp.stack(
        [
            padded[:, TILE * block_index : TILE * block_index + width_full]
            for block_index in range(block_count)
        ],
        0,
    )
    column_band = band_matrix(column_taps, width_full)
    column_pass = jnp.einsum(
        "jyw,kwt->kyjt", blocks, column_band, preferred_element_type=jnp.float32
    )
    column_pass = column_pass.reshape(NB, side_length, side_length).astype(jnp.bfloat16)
    row_padded = jnp.pad(column_pass, ((0, 0), (margin, margin), (0, 0)))
    row_blocks = jnp.stack(
        [
            row_padded[:, TILE * block_index : TILE * block_index + width_full, :]
            for block_index in range(block_count)
        ],
        0,
    )
    row_band = band_matrix(row_taps, width_full)
    summed = jnp.einsum("ikwx,kwt->itx", row_blocks, row_band, preferred_element_type=jnp.float32)
    return summed.reshape(side_length, side_length).astype(jnp.bfloat16)


def average_pieces(pieces):
    matched_in, weight_in = pieces
    weight_float = weight_in.astype(jnp.float32)
    numer = jnp.sum(weight_float * matched_in.astype(jnp.float32), axis=1)
    denom = jnp.sum(weight_float, axis=1)
    return (numer / jnp.maximum(denom, 1.0)).astype(jnp.bfloat16)


def subtract_template(template, matched, own_columns, side_length, sky_count):
    gathered = lax.all_gather(template, "sky", axis=1, tiled=True).reshape(
        side_length, sky_count, TILE
    )
    picked = jnp.take(gathered, own_columns, axis=1).reshape(side_length, side_length)
    return (matched.astype(jnp.float32) - picked.astype(jnp.float32)).astype(jnp.bfloat16)


def body(
    exposures,
    inv_variance,
    mask_planes,
    sky_columns,
    basis_rows,
    basis_cols,
    match_coeffs,
    detect_taps,
):
    picture = exposures[0, 0]
    side_length = picture.shape[0]
    block_count = side_length // TILE
    sky_count = lax.axis_size("sky")
    own_sky = lax.axis_index("sky")
    own_band = lax.axis_index("band")
    column_taps = (match_coeffs[0, 0][:, None] * basis_cols).astype(jnp.bfloat16)
    matched = psf_match(picture, column_taps, basis_rows.astype(jnp.bfloat16))
    keep = keep_pixels(mask_planes[0, 0], side_length)
    variance_inv = inv_variance[0, 0]
    weight = jnp.where(keep, variance_inv, jnp.zeros_like(variance_inv))
    own_columns = sky_columns[own_sky, own_band]
    empty_slots = jnp.zeros((side_length, sky_count, TILE), jnp.bfloat16)
    send_matched = empty_slots.at[:, own_columns, :].set(
        matched.reshape(side_length, block_count, TILE)
    )
    send_weight = empty_slots.at[:, own_columns, :].set(
        weight.reshape(side_length, block_count, TILE)
    )
    template = average_pieces(
        (
            lax.all_to_all(send_matched, "sky", split_axis=1, concat_axis=1, tiled=True),
            lax.all_to_all(send_weight, "sky", split_axis=1, concat_axis=1, tiled=True),
        )
    )
    difference = subtract_template(template, matched, own_columns, side_length, sky_count)
    margin = DTAPS // 2
    width_full = TILE + 2 * margin
    filter_band = band_matrix(detect_taps.astype(jnp.bfloat16), width_full)[0]
    widened = with_halo(template, (("sky", 1),), margin)
    smoothed = jnp.dot(widened, filter_band, preferred_element_type=jnp.float32).astype(
        jnp.bfloat16
    )
    smooth_padded = jnp.pad(smoothed, ((margin, margin), (0, 0)))
    smooth_blocks = jnp.stack(
        [
            smooth_padded[TILE * block_index : TILE * block_index + width_full]
            for block_index in range(block_count)
        ],
        0,
    )
    filtered = jnp.einsum(
        "iwx,wt->itx", smooth_blocks, filter_band, preferred_element_type=jnp.float32
    ).reshape(side_length, TILE)
    power = filtered * filtered
    detection = lax.psum_scatter(power, "band", scatter_dimension=0, tiled=True)
    return (difference[None, None], detection)


def solution(mesh):
    in_specs = (
        P("sky", "band", None, None),
        P("sky", "band", None, None),
        P("sky", "band", None, None),
        P(),
        P(),
        P(),
        P("sky", "band", None),
        P("band", None),
    )
    out_specs = (P("sky", "band", None, None), P("band", "sky"))
    return jax.shard_map(body, mesh=mesh, in_specs=in_specs, out_specs=out_specs, check_vma=False)
```

profile of v0, /device:TPU:0, one launch (start us, length us, event | category | flops | bytes accessed | tf_op | source)
XLA Modules:
  0.0 304.6 jit_solution(1016820240146248366)
XLA Ops:
  12.4 9.2 %convolution_convert_fusion = bf16[9,128,8,1024]{3,1,2,0:T(8,128)(2,1)} fusion(bf16[8,1024,152]{1,2,0:T(8,128)(2,1)S(1)} %fusion.34, bf16[9,152,128,1]{2,0,1,3:T(8,128)(2,1)S(1)} %fusion.19), kind=kOutput, calls=%fused_computation.5 | convolution fusion | flops 2878341120 | bytes 21714944 | tf_op jit(solution)/shard_map/jyw,kwt->kyjt/dot_general | solution.py:60
  21.6 24.6 %copy.67 = bf16[9,1024,1024]{2,1,0:T(8,128)(2,1)} copy(bf16[9,1024,1024]{1,2,0:T(8,128)(2,1)} %bitcast.237) | data formatting | bytes 37748736 | tf_op jit(solution)/shard_map/convert_element_type | solution.py:63
  46.3 4.3 %fusion.2 = bf16[8,9,152,1024]{3,2,1,0:T(8,128)(2,1)} fusion(bf16[9,1024,1024]{2,1,0:T(8,128)(2,1)} %copy.67), kind=kLoop, calls=%fused_computation.13 | loop fusion | bytes 21676032
  50.6 3.8 %copy-done = bf16[9,1024,1024]{2,1,0:T(8,128)(2,1)S(1)} copy-done((bf16[9,1024,1024]{2,1,0:T(8,128)(2,1)S(1)}, bf16[9,1024,1024]{2,1,0:T(8,128)(2,1)}, u32[]{:S(2)}) %copy-start) | copy-done | bytes 18874392
  72.2 9.9 %bitcast_convert_fusion = bf16[128,8,1024]{2,0,1:T(8,128)(2,1)S(1)} fusion(bf16[8,9,152,1024]{3,2,1,0:T(8,128)(2,1)} %fusion.4, bf16[9,152,128]{2,0,1:T(8,128)(2,1)S(1)} %fusion.20), kind=kOutput, calls=%fused_computation.9 | convolution fusion | flops 2869952512 | bytes 24860672 | tf_op jit(solution)/shard_map/ikwx,kwt->itx/dot_general | solution.py:73
  86.7 5.7 %scatter_fusion.1 = bf16[1024,8,128]{2,0,1:T(8,128)(2,1)} fusion(bf16[1024,8,128]{2,0,1:T(8,128)(2,1)} %broadcast_in_dim.16.clone.1, s32[8]{0:T(128)S(1)} %fusion.61, bf16[8,1024,128]{2,1,0:T(8,128)(2,1)} %bitcast.248), kind=kCustom, calls=%fused_computation.2 | custom fusion | bytes 6291488 | tf_op jit(solution)/shard_map/scatter | solution.py:116
  92.4 7.3 %all-to-all-start.1 = ((bf16[1024,8,128]{2,0,1:T(8,128)(2,1)}), bf16[1024,8,128]{2,0,1:T(8,128)(2,1)}, u32[]{:S(2)}, u32[]{:S(2)}) async-start(bf16[1024,8,128]{2,0,1:T(8,128)(2,1)} %scatter_fusion.1), calls=%async_computation.1 | async-start | bytes 4194304 | tf_op jit(solution)/shard_map/all_to_all | solution.py:124
  99.8 3.9 %copy.75 = bf16[1,1,1024,1024]{2,3,1,0:T(8,128)(2,1)} copy(bf16[1,1,1024,1024]{3,2,1,0:T(8,128)(2,1)} %param.9) | data formatting | bytes 4194304 | tf_op args[1]
  103.7 3.9 %copy.76 = bf16[1024,8,128]{2,0,1:T(8,128)(2,1)} copy(bf16[1024,8,128]{0,2,1:T(8,128)(2,1)} %bitcast.253) | data formatting | bytes 4194304 | tf_op jit(solution)/shard_map/squeeze | solution.py:112
  110.2 4.6 %compare_select_fusion.2 = s32[1024,1]{0,1:T(1,128)S(1)} fusion(s32[]{:T(128)} %bitcast.99, s32[]{:T(128)} %bitcast.100, s32[]{:T(128)} %bitcast.101, s32[]{:T(128)} %bitcast.102, s32[]{:T(128)} %bitcast.103, s32[]{:T(128)} %bitcast.105, s32[]{:T(128)} %bitcast.104), kind=kLoop, calls=%fused_computation.125 | loop fusion | flops 23552 | bytes 4124 | tf_op jit(solution)/shard_map/gather | solution.py:41
  116.3 4.4 %compare_select_fusion.1 = s32[1024,1]{0,1:T(1,128)S(1)} fusion(s32[]{:T(128)} %bitcast.63, s32[]{:T(128)} %bitcast.64, s32[]{:T(128)} %bitcast.65, s32[]{:T(128)} %bitcast.66, s32[]{:T(128)} %bitcast.67, s32[]{:T(128)} %bitcast.69, s32[]{:T(128)} %bitcast.68), kind=kLoop, calls=%fused_computation.124 | loop fusion | flops 23552 | bytes 4124 | tf_op jit(solution)/shard_map/gather | solution.py:42
  120.6 17.6 %fusion.49 = pred[8,128]{1,0:T(8,128)(4,1)S(1)} fusion(pred[1024]{0:T(1024)(128)(4,1)S(1)} %compare_reduce_fusion, pred[1024]{0:T(1024)(128)(4,1)S(1)} %compare_reduce_fusion.1, pred[1024]{0:T(1024)(128)(4,1)S(1)} %compare_reduce_fusion.2, pred[1024]{0:T(1024)(128)(4,1)S(1)} %compare_reduce_fusion.3, pred[1024]{0:T(1024)(128)(4,1)S(1)} %compare_reduce_fusion.4, ...), kind=kLoop, calls=%fused_computation.147 | loop fusion | flops 39936 | bytes 33904 | tf_op jit(solution)/shard_map/eq | solution.py:43
  138.3 17.6 %fusion.46 = pred[1024]{0:T(1024)(128)(4,1)S(1)} fusion(pred[1024]{0:T(1024)(128)(4,1)S(1)} %compare_reduce_fusion, pred[1024]{0:T(1024)(128)(4,1)S(1)} %compare_reduce_fusion.1, pred[1024]{0:T(1024)(128)(4,1)S(1)} %compare_reduce_fusion.2, pred[1024]{0:T(1024)(128)(4,1)S(1)} %compare_reduce_fusion.3, pred[1024]{0:T(1024)(128)(4,1)S(1)} %compare_reduce_fusion.4, ...), kind=kLoop, calls=%fused_computation.144 | loop fusion | flops 37888 | bytes 33904 | tf_op jit(solution)/shard_map/eq | solution.py:43
  155.9 3.6 %fusion.16 = bf16[8,1024,128]{2,1,0:T(8,128)(2,1)} fusion(bf16[1024,8,128]{2,0,1:T(8,128)(2,1)} %copy.76, pred[8,128]{1,0:T(8,128)(4,1)S(1)} %fusion.49, pred[1024]{0:T(1024)(128)(4,1)S(1)} %fusion.46), kind=kLoop, calls=%fused_computation.35 | loop fusion | flops 2097152 | bytes 4196352 | tf_op jit(solution)/shard_map/jit(_where)/select_n | solution.py:113
  161.1 5.7 %scatter_fusion = bf16[1024,8,128]{2,0,1:T(8,128)(2,1)} fusion(bf16[1024,8,128]{2,0,1:T(8,128)(2,1)} %broadcast_in_dim.16.clone, s32[8]{0:T(128)S(1)} %fusion.61, bf16[8,1024,128]{2,1,0:T(8,128)(2,1)} %fusion.16), kind=kCustom, calls=%fused_computation.1 | custom fusion | bytes 6291488 | tf_op jit(solution)/shard_map/scatter | solution.py:119
  166.8 53.7 %all_to_all.10 = bf16[1024,8,128]{2,0,1:T(8,128)(2,1)S(1)} all-to-all(bf16[1024,8,128]{2,0,1:T(8,128)(2,1)} %scatter_fusion), channel_id=1, replica_groups=mesh['sky'=8,'band'=4] {'sky'}, dimensions={1} | all-to-all | bytes 4194304 | tf_op jit(solution)/shard_map/all_to_all | solution.py:125
  226.9 3.3 %collective-permute-start.1 = (bf16[1024,15]{1,0:T(8,128)(2,1)S(1)}, bf16[1024,15]{1,0:T(8,128)(2,1)S(1)}, u32[]{:S(2)}, u32[]{:S(2)}) collective-permute-start(bf16[1024,15]{1,0:T(8,128)(2,1)S(1)} %get-tuple-element.11), channel_id=1, source_target_pairs={{4,0},{8,4},{12,8},{16,12},{20,16},{24,20},{28,24},{0,28},{5,1},{9... | collective-permute-start | bytes 92168 | tf_op jit(solution)/shard_map/ppermute | solution.py:21
  230.7 9.0 %collective-permute-done = bf16[1024,15]{1,0:T(8,128)(2,1)S(1)} collective-permute-done((bf16[1024,15]{1,0:T(8,128)(2,1)S(1)}, bf16[1024,15]{1,0:T(8,128)(2,1)S(1)}, u32[]{:S(2)}, u32[]{:S(2)}) %collective-permute-start) | collective-permute-done | bytes 30752 | tf_op jit(solution)/shard_map/ppermute | solution.py:18
  243.6 3.2 %copy.81 = f32[1,1,1024,1024]{2,3,1,0:T(8,128)} copy(bf16[1,1,1024,1024]{3,2,1,0:T(8,128)(2,1)S(1)} %bitcast.247) | data formatting | bytes 6291456 | tf_op jit(solution)/shard_map/convert_element_type | solution.py:90
  247.6 29.6 %all-gather.2.cloned.1.call-done = bf16[1024,1024]{1,0:T(8,128)(2,1)} async-done(((bf16[1024,128]{1,0:T(8,128)(2,1)}), bf16[1024,1024]{1,0:T(8,128)(2,1)}) %all-gather.2.cloned.1.call-update) | async-done | bytes 2097168 | tf_op jit(solution)/shard_map/all_gather | solution.py:86
  277.1 3.9 %copy.78 = bf16[1024,1024]{0,1:T(8,128)(2,1)} copy(bf16[1024,1024]{1,0:T(8,128)(2,1)} %all-gather.2.cloned.1.call-done) | data formatting | bytes 4194304 | tf_op jit(solution)/shard_map/all_gather | solution.py:86
  281.1 3.0 copy.79
  289.1 4.1 %subtract_convert_fusion = bf16[1,1,1024,1024]{2,3,1,0:T(8,128)(2,1)} fusion(f32[1,1,1024,1024]{2,3,1,0:T(8,128)} %copy.81, bf16[1,1,1024,1024]{2,3,1,0:T(8,128)(2,1)S(1)} %bitcast.249, pred[1024]{0:T(1024)(128)(4,1)S(1)} %broadcast_bitcast_fusion), kind=kLoop, calls=%fused_computation.10 | loop fusion | flops 4194304 | bytes 8389632 | tf_op jit(solution)/shard_map/convert_element_type | solution.py:90
  293.2 3.9 %copy.82 = bf16[1,1,1024,1024]{3,2,1,0:T(8,128)(2,1)} copy(bf16[1,1,1024,1024]{2,3,1,0:T(8,128)(2,1)} %subtract_convert_fusion) | data formatting | bytes 4194304
  (98 shorter events, 48.8 us)
Async XLA Ops:
  11.1 0.7 copy-start.3
  11.1 0.7 copy-start.4
  46.3 8.2 %copy-start = (bf16[9,1024,1024]{2,1,0:T(8,128)(2,1)S(1)}, bf16[9,1024,1024]{2,1,0:T(8,128)(2,1)}, u32[]{:S(2)}) copy-start(bf16[9,1024,1024]{2,1,0:T(8,128)(2,1)} %copy.67) | copy-start | bytes 56623108
  69.2 2.4 copy-start.5
  92.4 74.4 %all-to-all-start.1 = ((bf16[1024,8,128]{2,0,1:T(8,128)(2,1)}), bf16[1024,8,128]{2,0,1:T(8,128)(2,1)}, u32[]{:S(2)}, u32[]{:S(2)}) async-start(bf16[1024,8,128]{2,0,1:T(8,128)(2,1)} %scatter_fusion.1), calls=%async_computation.1 | async-start | bytes 4194304 | tf_op jit(solution)/shard_map/all_to_all | solution.py:124
  99.8 177.4 %all-gather.2.cloned.1.call-start = ((), (), s32[]{:S(2)}) async-start(), calls=%async_computation.3 | async-start | bytes 2359296 | tf_op jit(solution)/shard_map/all_gather | solution.py:86
  103.7 5.1 %copy-start.2 = (s32[1,1,2,35]{3,2,1,0:T(2,128)S(1)}, s32[1,1,2,35]{3,2,1,0:T(2,128)}, u32[]{:S(2)}) copy-start(s32[1,1,2,35]{3,2,1,0:T(2,128)} %param.10) | copy-start | bytes 844
  222.9 7.2 %copy-start.6 = (f32[1,31]{1,0:T(1,128)S(1)}, f32[1,31]{1,0:T(1,128)}, u32[]{:S(2)}) copy-start(f32[1,31]{1,0:T(1,128)} %param.15) | copy-start | bytes 376
  223.7 18.1 %copy-start.1 = (bf16[1024,128]{1,0:T(8,128)(2,1)S(1)}, bf16[1024,128]{1,0:T(8,128)(2,1)}, u32[]{:S(2)}) copy-start(bf16[1024,128]{1,0:T(8,128)(2,1)} %divide_convert_fusion) | copy-start | bytes 786436
  223.8 73.3 %reduce-scatter.2.cloned.1.call-start = ((), (), s32[]{:S(2)}) async-start(), calls=%async_computation.4 | async-start | bytes 655360 | tf_op jit(solution)/shard_map/reduce_scatter | solution.py:148
  225.3 14.3 %collective-permute-start = (bf16[1024,15]{1,0:T(8,128)(2,1)S(1)}, bf16[1024,15]{1,0:T(8,128)(2,1)S(1)}, u32[]{:S(2)}, u32[]{:S(2)}) collective-permute-start(bf16[1024,15]{1,0:T(8,128)(2,1)S(1)} %get-tuple-element.10), channel_id=1, source_target_pairs={{0,4},{4,8},{8,12},{12,16},{16,20},{20,24},{24,28},{28,0},{1,5},{5... | collective-permute-start | bytes 92168 | tf_op jit(solution)/shard_map/ppermute | solution.py:18
  226.9 15.0 %collective-permute-start.1 = (bf16[1024,15]{1,0:T(8,128)(2,1)S(1)}, bf16[1024,15]{1,0:T(8,128)(2,1)S(1)}, u32[]{:S(2)}, u32[]{:S(2)}) collective-permute-start(bf16[1024,15]{1,0:T(8,128)(2,1)S(1)} %get-tuple-element.11), channel_id=1, source_target_pairs={{4,0},{8,4},{12,8},{16,12},{20,16},{24,20},{28,24},{0,28},{5,1},{9... | collective-permute-start | bytes 92168 | tf_op jit(solution)/shard_map/ppermute | solution.py:21
Sparse Core Ops, SparseCore 0:
  223.9 53.1 all-gather.1
Sparse Core Ops, SparseCore 1:
  243.6 20.2 reduce-scatter.1
where the time goes:
time: 307 us; the launch traced here: 305 us
  local copies, waits for them, and re-layouts  102 us (33%)
  other arithmetic  57.9 us (19%)
  blocking collectives  53.7 us (17%)
  waiting for transfers between devices  40.8 us (13%)
  matrix products  22.3 us (7%)
  between operations  15.7 us (5%)
  starting transfers between devices  12.2 us (4%)
    all_to_all x1, blocking collectives, body(): lax.all_to_all(send_weight, 'sky', split_axis=1, concat_axis=1, tiled=True)  53.7 us
    unnamed x39, local copies, waits for them, and re-layouts  35.3 us
    eq x2, other arithmetic, keep_pixels(): return jnp.logical_and(row_bits[:, None] == 0, column_bits[None, :] == 0)  35.2 us
    all_gather x1, waiting for transfers between devices, subtract_template(): lax.all_gather(template, 'sky', axis=1, tiled=True)  29.6 us
    convert_element_type x1, local copies, waits for them, and re-layouts, psf_match(): column_pass.reshape(NB, side_length, side_length).astype(jnp.bfloat16)  24.6 us
    scatter x2, local copies, waits for them, and re-layouts, body(): empty_slots.at[:, own_columns, :]  11.4 us
    dot_general x1, matrix products, psf_match(): jnp.einsum('ikwx,kwt->itx', row_blocks, row_band, preferred_element_type=...  9.89 us
    dot_general x1, matrix products, psf_match(): jnp.einsum('jyw,kwt->kyjt', blocks, column_band, preferred_element_type=j...  9.18 us
  transfers between devices with their start and end apart: 5, of which 3 were waited for; matrix products, arithmetic and copies ran while one was open for 31% of the time, Pallas kernels for 0%

commit v1 on v0

--- a/solution.py
+++ b/solution.py
@@ -83,7 +83,7 @@
 
 
 def subtract_template(template, matched, own_columns, side_length, sky_count):
-    gathered = lax.all_gather(template, "sky", axis=1, tiled=True).reshape(
+    gathered = jnp.concatenate(lax.all_gather(template, "sky"), axis=1).reshape(
         side_length, sky_count, TILE
     )
     picked = jnp.take(gathered, own_columns, axis=1).reshape(side_length, side_length)

time: 307 us -> 300 us (0.977)
  local copies, waits for them, and re-layouts: 102 us -> 96.4 us
    all_gather x1 -> x0, local copies, waits for them, and re-layouts: 3.93 us -> none  [subtract_template(): lax.all_gather(template, 'sky', axis=1, tiled=True)]
  transfers between devices with their start and end apart: 5 -> 5, of which waited for: 3 -> 3; matrix products, arithmetic and copies ran while one was open for 31% -> 30% of each run, Pallas kernels for 0% -> 0%
where the time goes in v1:
time: 300 us; the launch traced here: 298 us
  local copies, waits for them, and re-layouts  96.4 us (32%)
  other arithmetic  57.9 us (19%)
  blocking collectives  53.7 us (18%)
  waiting for transfers between devices  39.5 us (13%)
  matrix products  22.3 us (7%)
  between operations  15.7 us (5%)
  starting transfers between devices  12.2 us (4%)
    all_to_all x1, blocking collectives, body(): lax.all_to_all(send_weight, 'sky', split_axis=1, concat_axis=1, tiled=True)  53.7 us
    unnamed x39, local copies, waits for them, and re-layouts  35.3 us
    eq x2, other arithmetic, keep_pixels(): return jnp.logical_and(row_bits[:, None] == 0, column_bits[None, :] == 0)  35.2 us
    all_gather x1, waiting for transfers between devices, subtract_template(): lax.all_gather(template, 'sky')  28.3 us
    convert_element_type x1, local copies, waits for them, and re-layouts, psf_match(): column_pass.reshape(NB, side_length, side_length).astype(jnp.bfloat16)  24.6 us
    scatter x2, local copies, waits for them, and re-layouts, body(): empty_slots.at[:, own_columns, :]  11.4 us
    dot_general x1, matrix products, psf_match(): jnp.einsum('ikwx,kwt->itx', row_blocks, row_band, preferred_element_type=...  9.89 us
    dot_general x1, matrix products, psf_match(): jnp.einsum('jyw,kwt->kyjt', blocks, column_band, preferred_element_type=j...  9.18 us
  transfers between devices with their start and end apart: 5, of which 3 were waited for; matrix products, arithmetic and copies ran while one was open for 30% of the time, Pallas kernels for 0%

profile of v1, /device:TPU:0, one launch (start us, length us, event | category | flops | bytes accessed | tf_op | source)
XLA Modules:
  0.0 297.7 jit_solution(8054220407176057670)
XLA Ops:
  8.0 2.9 copy.46
  12.4 9.2 %convolution_convert_fusion = bf16[9,128,8,1024]{3,1,2,0:T(8,128)(2,1)} fusion(bf16[8,1024,152]{1,2,0:T(8,128)(2,1)S(1)} %fusion.34, bf16[9,152,128,1]{2,0,1,3:T(8,128)(2,1)S(1)} %fusion.19), kind=kOutput, calls=%fused_computation.5 | convolution fusion | flops 2878341120 | bytes 21714944 | tf_op jit(solution)/shard_map/jyw,kwt->kyjt/dot_general | solution.py:60
  21.6 24.6 %copy.48 = bf16[9,1024,1024]{2,1,0:T(8,128)(2,1)} copy(bf16[9,1024,1024]{1,2,0:T(8,128)(2,1)} %bitcast.239) | data formatting | bytes 37748736 | tf_op jit(solution)/shard_map/convert_element_type | solution.py:63
  46.3 4.3 %fusion.2 = bf16[8,9,152,1024]{3,2,1,0:T(8,128)(2,1)} fusion(bf16[9,1024,1024]{2,1,0:T(8,128)(2,1)} %copy.48), kind=kLoop, calls=%fused_computation.13 | loop fusion | bytes 21676032
  50.6 3.8 %copy-done = bf16[9,1024,1024]{2,1,0:T(8,128)(2,1)S(1)} copy-done((bf16[9,1024,1024]{2,1,0:T(8,128)(2,1)S(1)}, bf16[9,1024,1024]{2,1,0:T(8,128)(2,1)}, u32[]{:S(2)}) %copy-start) | copy-done | bytes 18874392
  72.2 9.9 %bitcast_convert_fusion = bf16[128,8,1024]{2,0,1:T(8,128)(2,1)S(1)} fusion(bf16[8,9,152,1024]{3,2,1,0:T(8,128)(2,1)} %fusion.4, bf16[9,152,128]{2,0,1:T(8,128)(2,1)S(1)} %fusion.20), kind=kOutput, calls=%fused_computation.9 | convolution fusion | flops 2869952512 | bytes 24860672 | tf_op jit(solution)/shard_map/ikwx,kwt->itx/dot_general | solution.py:73
  86.7 5.7 %scatter_fusion.1 = bf16[1024,8,128]{2,0,1:T(8,128)(2,1)} fusion(bf16[1024,8,128]{2,0,1:T(8,128)(2,1)} %broadcast_in_dim.16.clone.1, s32[8]{0:T(128)S(1)} %fusion.61, bf16[8,1024,128]{2,1,0:T(8,128)(2,1)} %bitcast.250), kind=kCustom, calls=%fused_computation.2 | custom fusion | bytes 6291488 | tf_op jit(solution)/shard_map/scatter | solution.py:116
  92.4 7.3 %all-to-all-start.1 = ((bf16[1024,8,128]{2,0,1:T(8,128)(2,1)}), bf16[1024,8,128]{2,0,1:T(8,128)(2,1)}, u32[]{:S(2)}, u32[]{:S(2)}) async-start(bf16[1024,8,128]{2,0,1:T(8,128)(2,1)} %scatter_fusion.1), calls=%async_computation.1 | async-start | bytes 4194304 | tf_op jit(solution)/shard_map/all_to_all | solution.py:124
  99.8 3.9 %copy.56 = bf16[1,1,1024,1024]{2,3,1,0:T(8,128)(2,1)} copy(bf16[1,1,1024,1024]{3,2,1,0:T(8,128)(2,1)} %param.9) | data formatting | bytes 4194304 | tf_op args[1]
  103.7 3.9 %copy.57 = bf16[1024,8,128]{2,0,1:T(8,128)(2,1)} copy(bf16[1024,8,128]{0,2,1:T(8,128)(2,1)} %bitcast.254) | data formatting | bytes 4194304 | tf_op jit(solution)/shard_map/squeeze | solution.py:112
  110.2 4.6 %compare_select_fusion.2 = s32[1024,1]{0,1:T(1,128)S(1)} fusion(s32[]{:T(128)} %bitcast.99, s32[]{:T(128)} %bitcast.100, s32[]{:T(128)} %bitcast.101, s32[]{:T(128)} %bitcast.102, s32[]{:T(128)} %bitcast.103, s32[]{:T(128)} %bitcast.105, s32[]{:T(128)} %bitcast.104), kind=kLoop, calls=%fused_computation.125 | loop fusion | flops 23552 | bytes 4124 | tf_op jit(solution)/shard_map/gather | solution.py:41
  116.3 4.4 %compare_select_fusion.1 = s32[1024,1]{0,1:T(1,128)S(1)} fusion(s32[]{:T(128)} %bitcast.63, s32[]{:T(128)} %bitcast.64, s32[]{:T(128)} %bitcast.65, s32[]{:T(128)} %bitcast.66, s32[]{:T(128)} %bitcast.67, s32[]{:T(128)} %bitcast.69, s32[]{:T(128)} %bitcast.68), kind=kLoop, calls=%fused_computation.124 | loop fusion | flops 23552 | bytes 4124 | tf_op jit(solution)/shard_map/gather | solution.py:42
  120.6 17.6 %fusion.49 = pred[8,128]{1,0:T(8,128)(4,1)S(1)} fusion(pred[1024]{0:T(1024)(128)(4,1)S(1)} %compare_reduce_fusion, pred[1024]{0:T(1024)(128)(4,1)S(1)} %compare_reduce_fusion.1, pred[1024]{0:T(1024)(128)(4,1)S(1)} %compare_reduce_fusion.2, pred[1024]{0:T(1024)(128)(4,1)S(1)} %compare_reduce_fusion.3, pred[1024]{0:T(1024)(128)(4,1)S(1)} %compare_reduce_fusion.4, ...), kind=kLoop, calls=%fused_computation.147 | loop fusion | flops 39936 | bytes 33904 | tf_op jit(solution)/shard_map/eq | solution.py:43
  138.3 17.6 %fusion.46 = pred[1024]{0:T(1024)(128)(4,1)S(1)} fusion(pred[1024]{0:T(1024)(128)(4,1)S(1)} %compare_reduce_fusion, pred[1024]{0:T(1024)(128)(4,1)S(1)} %compare_reduce_fusion.1, pred[1024]{0:T(1024)(128)(4,1)S(1)} %compare_reduce_fusion.2, pred[1024]{0:T(1024)(128)(4,1)S(1)} %compare_reduce_fusion.3, pred[1024]{0:T(1024)(128)(4,1)S(1)} %compare_reduce_fusion.4, ...), kind=kLoop, calls=%fused_computation.144 | loop fusion | flops 37888 | bytes 33904 | tf_op jit(solution)/shard_map/eq | solution.py:43
  155.9 3.6 %fusion.16 = bf16[8,1024,128]{2,1,0:T(8,128)(2,1)} fusion(bf16[1024,8,128]{2,0,1:T(8,128)(2,1)} %copy.57, pred[8,128]{1,0:T(8,128)(4,1)S(1)} %fusion.49, pred[1024]{0:T(1024)(128)(4,1)S(1)} %fusion.46), kind=kLoop, calls=%fused_computation.35 | loop fusion | flops 2097152 | bytes 4196352 | tf_op jit(solution)/shard_map/jit(_where)/select_n | solution.py:113
  161.1 5.7 %scatter_fusion = bf16[1024,8,128]{2,0,1:T(8,128)(2,1)} fusion(bf16[1024,8,128]{2,0,1:T(8,128)(2,1)} %broadcast_in_dim.16.clone, s32[8]{0:T(128)S(1)} %fusion.61, bf16[8,1024,128]{2,1,0:T(8,128)(2,1)} %fusion.16), kind=kCustom, calls=%fused_computation.1 | custom fusion | bytes 6291488 | tf_op jit(solution)/shard_map/scatter | solution.py:119
  166.8 53.7 %all_to_all.10 = bf16[1024,8,128]{2,0,1:T(8,128)(2,1)S(1)} all-to-all(bf16[1024,8,128]{2,0,1:T(8,128)(2,1)} %scatter_fusion), channel_id=1, replica_groups=mesh['sky'=8,'band'=4] {'sky'}, dimensions={1} | all-to-all | bytes 4194304 | tf_op jit(solution)/shard_map/all_to_all | solution.py:125
  226.9 3.3 %collective-permute-start.1 = (bf16[1024,15]{1,0:T(8,128)(2,1)S(1)}, bf16[1024,15]{1,0:T(8,128)(2,1)S(1)}, u32[]{:S(2)}, u32[]{:S(2)}) collective-permute-start(bf16[1024,15]{1,0:T(8,128)(2,1)S(1)} %get-tuple-element.9), channel_id=1, source_target_pairs={{4,0},{8,4},{12,8},{16,12},{20,16},{24,20},{28,24},{0,28},{5,1},{9... | collective-permute-start | bytes 92168 | tf_op jit(solution)/shard_map/ppermute | solution.py:21
  230.7 9.0 %collective-permute-done = bf16[1024,15]{1,0:T(8,128)(2,1)S(1)} collective-permute-done((bf16[1024,15]{1,0:T(8,128)(2,1)S(1)}, bf16[1024,15]{1,0:T(8,128)(2,1)S(1)}, u32[]{:S(2)}, u32[]{:S(2)}) %collective-permute-start) | collective-permute-done | bytes 30752 | tf_op jit(solution)/shard_map/ppermute | solution.py:18
  243.6 3.0 %copy.60 = f32[1,1,1024,1024]{2,3,1,0:T(8,128)} copy(bf16[1,1,1024,1024]{3,2,1,0:T(8,128)(2,1)S(1)} %bitcast.249) | data formatting | bytes 6291456 | tf_op jit(solution)/shard_map/convert_element_type | solution.py:90
  247.4 28.3 %all-gather.3.cloned.1.call-done = bf16[8192,128]{1,0:T(8,128)(2,1)} async-done(((bf16[1024,128]{1,0:T(8,128)(2,1)}), bf16[8192,128]{1,0:T(8,128)(2,1)}) %all-gather.3.cloned.1.call-update) | async-done | bytes 2097168 | tf_op jit(solution)/shard_map/all_gather | solution.py:86
  275.6 3.7 %gather_fusion = bf16[8,1024,128]{2,1,0:T(8,128)(2,1)} fusion(bf16[1024,8,128]{2,0,1:T(8,128)(2,1)} %bitcast.256, s32[1024]{0:T(1024)S(1)} %pad_clamp_fusion), kind=kCustom, calls=%fused_computation | custom fusion | bytes 4194336 | tf_op jit(solution)/shard_map/jit(_take)/gather | solution.py:89
  282.2 4.1 %subtract_convert_fusion = bf16[1,1,1024,1024]{2,3,1,0:T(8,128)(2,1)} fusion(f32[1,1,1024,1024]{2,3,1,0:T(8,128)} %copy.60, bf16[1,1,1024,1024]{2,3,1,0:T(8,128)(2,1)S(1)} %bitcast.251, pred[1024]{0:T(1024)(128)(4,1)S(1)} %broadcast_bitcast_fusion), kind=kLoop, calls=%fused_computation.10 | loop fusion | flops 4194304 | bytes 8389632 | tf_op jit(solution)/shard_map/convert_element_type | solution.py:90
  286.3 3.9 %copy.61 = bf16[1,1,1024,1024]{3,2,1,0:T(8,128)(2,1)} copy(bf16[1,1,1024,1024]{2,3,1,0:T(8,128)(2,1)} %subtract_convert_fusion) | data formatting | bytes 4194304
  (96 shorter events, 43.8 us)
Async XLA Ops:
  11.1 0.7 copy-start.3
  11.1 0.7 copy-start.4
  46.3 8.2 %copy-start = (bf16[9,1024,1024]{2,1,0:T(8,128)(2,1)S(1)}, bf16[9,1024,1024]{2,1,0:T(8,128)(2,1)}, u32[]{:S(2)}) copy-start(bf16[9,1024,1024]{2,1,0:T(8,128)(2,1)} %copy.48) | copy-start | bytes 56623108
  69.2 2.4 copy-start.5
  92.4 74.4 %all-to-all-start.1 = ((bf16[1024,8,128]{2,0,1:T(8,128)(2,1)}), bf16[1024,8,128]{2,0,1:T(8,128)(2,1)}, u32[]{:S(2)}, u32[]{:S(2)}) async-start(bf16[1024,8,128]{2,0,1:T(8,128)(2,1)} %scatter_fusion.1), calls=%async_computation.1 | async-start | bytes 4194304 | tf_op jit(solution)/shard_map/all_to_all | solution.py:124
  99.8 175.9 %all-gather.3.cloned.1.call-start = ((), (), s32[]{:S(2)}) async-start(), calls=%async_computation.4 | async-start | bytes 2359296 | tf_op jit(solution)/shard_map/all_gather | solution.py:86
  103.7 5.1 %copy-start.2 = (s32[1,1,2,35]{3,2,1,0:T(2,128)S(1)}, s32[1,1,2,35]{3,2,1,0:T(2,128)}, u32[]{:S(2)}) copy-start(s32[1,1,2,35]{3,2,1,0:T(2,128)} %param.10) | copy-start | bytes 844
  222.9 7.2 %copy-start.6 = (f32[1,31]{1,0:T(1,128)S(1)}, f32[1,31]{1,0:T(1,128)}, u32[]{:S(2)}) copy-start(f32[1,31]{1,0:T(1,128)} %param.15) | copy-start | bytes 376
  223.7 18.1 %copy-start.1 = (bf16[1024,128]{1,0:T(8,128)(2,1)S(1)}, bf16[1024,128]{1,0:T(8,128)(2,1)}, u32[]{:S(2)}) copy-start(bf16[1024,128]{1,0:T(8,128)(2,1)} %divide_convert_fusion) | copy-start | bytes 786436
  223.8 66.4 %reduce-scatter.2.cloned.1.call-start = ((), (), s32[]{:S(2)}) async-start(), calls=%async_computation.3 | async-start | bytes 655360 | tf_op jit(solution)/shard_map/reduce_scatter | solution.py:148
  225.3 14.3 %collective-permute-start = (bf16[1024,15]{1,0:T(8,128)(2,1)S(1)}, bf16[1024,15]{1,0:T(8,128)(2,1)S(1)}, u32[]{:S(2)}, u32[]{:S(2)}) collective-permute-start(bf16[1024,15]{1,0:T(8,128)(2,1)S(1)} %get-tuple-element.8), channel_id=1, source_target_pairs={{0,4},{4,8},{8,12},{12,16},{16,20},{20,24},{24,28},{28,0},{1,5},{5... | collective-permute-start | bytes 92168 | tf_op jit(solution)/shard_map/ppermute | solution.py:18
  226.9 15.0 %collective-permute-start.1 = (bf16[1024,15]{1,0:T(8,128)(2,1)S(1)}, bf16[1024,15]{1,0:T(8,128)(2,1)S(1)}, u32[]{:S(2)}, u32[]{:S(2)}) collective-permute-start(bf16[1024,15]{1,0:T(8,128)(2,1)S(1)} %get-tuple-element.9), channel_id=1, source_target_pairs={{4,0},{8,4},{12,8},{16,12},{20,16},{24,20},{28,24},{0,28},{5,1},{9... | collective-permute-start | bytes 92168 | tf_op jit(solution)/shard_map/ppermute | solution.py:21
Sparse Core Ops, SparseCore 0:
  223.9 51.6 all-gather.2
Sparse Core Ops, SparseCore 1:
  243.6 20.2 reduce-scatter.1
